TPU v7x, 128 devices: a whole 4x4x4 slice. The times are simulated.
128 devices in a mesh: row: 8 (over x_hi, z), col: 16 (over y, x_lo, core).
Axes of the slice: x: 4 (x_hi: 2, x_lo: 2; x = x_hi * 2 + x_lo), y: 4, z: 4, core: 2. Of those that a mesh axis runs over, the one named last changes fastest.
Arguments:
- positions: float32 [1024, 24576], P('row', 'col'), may hold values from -2.5 to 2.5
- momenta: float32 [1024, 24576], P('row', 'col'), may hold values from -2.5 to 2.5
- couplings: float32 [24576, 24576], P('row', 'col'), may hold values from -0.0390625 to 0.0390625
Outputs:
- positions_next: float32 [1024, 24576], P('row', 'col')
- momenta_next: float32 [1024, 24576], P('row', 'col')
All inputs are finite; a program needn't handle non-finite values.
Results may differ from a plain program's by a relative error of at most 0.00005.
Values sent between devices are 32-bit elements; how exact they have to be, the bound alone decides.
A program may use at most 128 MiB of HBM per device.

v0:
```python
import jax
import jax.numpy as jnp
from jax import lax
from jax.sharding import PartitionSpec as P

time_step = 0.5
kerr_rate = 1.0
pump_rate = 0.6
detuning = 0.4
coupling_gain = 1.5


def from_root(x, axis, root):
    mine = lax.axis_index(axis) == root
    return lax.psum(jnp.where(mine, x, jnp.zeros_like(x)), axis)


def column_blocks(positions):
    return lax.all_gather(positions, "row", axis=0, tiled=True)


def per_device(positions, momenta, couplings):
    row_index = lax.axis_index("row")
    root_col = 2 * row_index
    column_block = column_blocks(positions)
    first_half = from_root(column_block, "col", root_col)
    second_half = from_root(column_block, "col", root_col + 1)
    gathered = jnp.concatenate([first_half, second_half], axis=1)
    partial_force = jnp.dot(
        gathered, couplings, precision=lax.Precision.HIGHEST, preferred_element_type=jnp.float32
    )
    coupled = lax.psum_scatter(partial_force, "row", scatter_dimension=0, tiled=True)
    radius = positions * positions + momenta * momenta
    momenta_next = momenta + time_step * (
        -(kerr_rate * radius - pump_rate + detuning) * positions + coupling_gain * coupled
    )
    radius_next = positions * positions + momenta_next * momenta_next
    positions_next = (
        positions + time_step * (kerr_rate * radius_next + pump_rate + detuning) * momenta_next
    )
    return (positions_next, momenta_next)


def solution(mesh):
    placed = (P("row", "col"), P("row", "col"), P("row", "col"))
    return jax.shard_map(
        per_device,
        mesh=mesh,
        in_specs=placed,
        out_specs=(P("row", "col"), P("row", "col")),
        check_vma=False,
    )
```

profile of v0, /device:TPU:0, one launch (start us, length us, event | category | flops | bytes accessed | tf_op | source)
XLA Modules:
  0.0 560.3 jit_solution(7543965145673670952)
XLA Ops:
  7.2 0.0 all-gather.2.cloned.1.call-start
  7.2 0.7 all-gather.2.cloned.1.call-update
  7.9 0.0 all-reduce.3.cloned.1.call-start
  8.0 93.6 %all-gather.2.cloned.1.call-done = f32[1024,1536]{1,0:T(8,128)} async-done(((f32[128,1536]{1,0:T(8,128)}), f32[1024,1536]{1,0:T(8,128)}) %all-gather.2.cloned.1.call-update) | async-done | bytes 6291472 | tf_op jit(solution)/shard_map/all_gather | solution.py:19
  101.5 9.0 %broadcast_select_fusion.1 = (f32[1024,1536]{1,0:T(8,128)}, f32[1024,1536]{1,0:T(8,128)}) fusion(f32[1024,1536]{1,0:T(8,128)} %all-gather.2.cloned.1.call-done, pred[]{:T(512)S(6)} %eq.6, pred[]{:T(512)S(6)} %eq.7), kind=kLoop, calls=%fused_computation.5 | loop fusion | flops 3145728 | bytes 18874370 | tf_op jit(solution)/shard_map/jit(_where)/select_n | solution.py:15
  110.6 0.0 all-reduce.3.cloned.1.call-update
  110.6 0.0 reduce-scatter.2.cloned.1.call-start
  110.6 276.9 %all-reduce.3.cloned.1.call-done = (f32[1024,1536]{1,0:T(8,128)}, f32[1024,1536]{1,0:T(8,128)}) async-done(((f32[1024,1536]{1,0:T(8,128)}, f32[1024,1536]{1,0:T(8,128)}), (f32[1024,1536]{1,0:T(8,128)}, f32[1024,1536]{1,0:T(8,128)})) %all-reduce.3.cloned.1.call-update) | async-done | bytes 12582928 | tf_op jit(solution)/shard_map/psum | solution.py:15
  387.5 66.4 %fusion = f32[1024,1536]{1,0:T(8,128)} fusion(f32[3072,1536]{1,0:T(8,128)} %param.5, f32[1024,1536]{1,0:T(8,128)} %get-tuple-element.2, f32[1024,1536]{1,0:T(8,128)} %get-tuple-element.3), kind=kOutput, calls=%fused_computation | convolution fusion | flops 57985204224 | bytes 37748736 | tf_op jit(solution)/shard_map/dot_general | solution.py:29
  453.9 0.0 copy-start
  453.9 0.0 copy-start.1
  453.9 0.0 reduce-scatter.2.cloned.1.call-update
  453.9 97.2 %reduce-scatter.2.cloned.1.call-done = f32[128,1536]{1,0:T(8,128)} async-done(((f32[1024,1536]{1,0:T(8,128)}), f32[128,1536]{1,0:T(8,128)}) %reduce-scatter.2.cloned.1.call-update) | async-done | bytes 786448 | tf_op jit(solution)/shard_map/reduce_scatter | solution.py:32
  551.1 0.0 copy-done
  551.1 0.0 copy-done.1
  551.1 2.7 multiply_add_fusion
Async XLA Ops:
  7.2 94.4 %all-gather.2.cloned.1.call-start = ((), (), s32[]{:S(2)}) async-start(), calls=%async_computation.1 | async-start | bytes 7077888 | tf_op jit(solution)/shard_map/all_gather | solution.py:19
  7.9 379.6 %all-reduce.3.cloned.1.call-start = ((), (), s32[]{:S(2)}) async-start(), calls=%async_computation.3 | async-start | bytes 25165824 | tf_op jit(solution)/shard_map/psum | solution.py:15
  110.6 440.5 %reduce-scatter.2.cloned.1.call-start = ((), (), s32[]{:S(2)}) async-start(), calls=%async_computation.2 | async-start | bytes 7077888 | tf_op jit(solution)/shard_map/reduce_scatter | solution.py:32
  453.9 97.2 %copy-start = (f32[128,1536]{1,0:T(8,128)S(1)}, f32[128,1536]{1,0:T(8,128)}, u32[]{:S(2)}) copy-start(f32[128,1536]{1,0:T(8,128)} %param.3) | copy-start | bytes 2359300
  453.9 97.2 %copy-start.1 = (f32[128,1536]{1,0:T(8,128)S(1)}, f32[128,1536]{1,0:T(8,128)}, u32[]{:S(2)}) copy-start(f32[128,1536]{1,0:T(8,128)} %param.4) | copy-start | bytes 2359300
Sparse Core Ops, SparseCore 0:
  10.3 91.2 all-gather.1
  110.7 276.7 all-reduce.2
  454.0 97.0 reduce-scatter.1
where the time goes:
time: 561 us; the launch traced here: 560 us
  waiting for transfers between devices  468 us (83%)
  matrix products  66.4 us (12%)
  between operations  13.8 us (2%)
  other arithmetic  11.7 us (2%)
    psum x1, waiting for transfers between devices, from_root(): return lax.psum(jnp.where(mine, x, jnp.zeros_like(x)), axis)  277 us
    reduce_scatter x1, waiting for transfers between devices, per_device(): lax.psum_scatter(partial_force, 'row', scatter_dimension=0, tiled=True)  97.2 us
    all_gather x1, waiting for transfers between devices, column_blocks(): return lax.all_gather(positions, 'row', axis=0, tiled=True)  93.6 us
    dot_general x1, matrix products, per_device(): jnp.dot(gathered, couplings, precision=lax.Precision.HIGHEST, preferred_e...  66.4 us
  transfers between devices with their start and end apart: 3, of which 3 were waited for; matrix products, arithmetic and copies ran while one was open for 0% of the time, Pallas kernels for 0%

commit v1 on v0

v1 whole, which is shorter than its diff:
```python
import jax
import jax.numpy as jnp
from jax import lax
from jax.experimental import pallas as pl
from jax.experimental.pallas import tpu as pltpu
from jax.sharding import PartitionSpec as P

time_step = 0.5
kerr_rate = 1.0
pump_rate = 0.6
detuning = 0.4
coupling_gain = 1.5

MESH = pl.DeviceIdType.MESH
BF16 = jnp.bfloat16
F32 = jnp.float32
CHUNKS = 8
PIECE = 384
TILE = 512
(T, XL, UP, UP2, DN, DN2, UPR, DNR, SWAP, ZP, ZM, FP0, FP1, FM0, FM1, XH) = range(16)


def slot_of(a, b):
    xh, z = a // 4, a % 4
    y, xl = b // 2, b % 2
    return 2 * ((z + 2 * y + xl) % 4) + (xh + z // 2) % 2


def kernel(
    pos, coup, out, xg, jhi, jlo, stage, x2, p, rzp, rzm, rfp, rfm, rx, send, recv, stage_sem
):
    n, _, _, m, width = xg.shape
    row, col = lax.axis_index("row"), lax.axis_index("col")
    xh, z = row // 4, row % 4
    core = col % 2
    slot = col // 2
    y, xl = slot // 2, slot % 2
    up, down = (y + 1) % 4, (y + 3) % 4
    zup, zdown, zfar = (z + 1) % 4, (z + 3) % 4, (z + 2) % 4

    def at(row_, y_, xl_, core_):
        return {"row": row_, "col": (2 * y_ + xl_) * 2 + core_}

    t_slot = slot_of(row, slot)
    t_to = {"row": slot, "col": t_slot * 2 + core}
    own = jnp.logical_and(slot == row, t_slot == slot)
    t_from = 0
    for a in range(8):
        t_from = t_from + jnp.where(slot_of(jnp.int32(a), row) == slot, a, 0)
    side = at(row, y, 1 - xl, core)
    above, below = at(row, up, xl, core), at(row, down, xl, core)
    twin = at(row, y, xl, 1 - core)
    zabove, zbelow = at(4 * xh + zup, y, xl, core), at(4 * xh + zdown, y, xl, core)
    across = at(4 * (1 - xh) + z, y, xl, core)

    pieces = coup.shape[0] // PIECE

    def piece_copy(q):
        rows = pl.ds(pl.multiple_of(q * PIECE, PIECE), PIECE)
        return pltpu.make_async_copy(coup.at[rows], stage.at[q % 2], stage_sem.at[q % 2])

    piece_copy(0).start()
    piece_copy(1).start()

    barrier = pltpu.get_barrier_semaphore()
    for other in (side, above, below, twin, zabove, zbelow, across):
        pl.semaphore_signal(barrier, inc=1, device_id=other, device_id_type=MESH)

    @pl.when(jnp.logical_not(own))
    def _():
        pl.semaphore_signal(
            barrier, inc=1, device_id={"row": t_from, "col": row * 2 + core}, device_id_type=MESH
        )
        pl.semaphore_wait(barrier, 8)

    @pl.when(own)
    def _():
        pl.semaphore_wait(barrier, 7)

    def remote(kind, i, src, dst, to):
        return pltpu.make_async_remote_copy(
            src_ref=src,
            dst_ref=dst,
            send_sem=send.at[kind, i],
            recv_sem=recv.at[kind, i],
            device_id=to,
            device_id_type=MESH,
        )

    def rows_of(i, a):
        return p.at[i, pl.ds(pl.multiple_of(a * m, m), m)]

    def t_src(i):
        return pos.at[pl.ds(pl.multiple_of(i * m, m), m)]

    def t_copy(i):
        return remote(T, i, t_src(i), xg.at[i, core, t_slot], t_to)

    def t_local(i):
        return pltpu.make_async_copy(t_src(i), xg.at[i, core, slot], recv.at[T, i])

    def gather_copy(kind, i, slot_, to):
        block = xg.at[i, core, slot_]
        return remote(kind, i, block, block, to)

    def gather_copies(i):
        return {
            XL: lambda: gather_copy(XL, i, slot, side),
            UP: lambda: gather_copy(UP, i, slot, above),
            DN: lambda: gather_copy(DN, i, slot, below),
            UP2: lambda: gather_copy(UP2, i, 2 * y + 1 - xl, above),
            DN2: lambda: gather_copy(DN2, i, 2 * y + 1 - xl, below),
            UPR: lambda: gather_copy(UPR, i, 2 * down + xl, above),
            DNR: lambda: gather_copy(DNR, i, 2 * up + 1 - xl, below),
            SWAP: lambda: remote(SWAP, i, xg.at[i, core], xg.at[i, core], twin),
        }

    def sum_copies(i):
        return {
            ZP: lambda: remote(ZP, i, rows_of(i, zfar), rzp.at[i], zabove),
            ZM: lambda: remote(ZM, i, rows_of(i, 4 + zfar), rzm.at[i], zbelow),
            FP0: lambda: remote(FP0, i, rows_of(i, zup), rfp.at[i, 0], zabove),
            FP1: lambda: remote(FP1, i, rows_of(i, 4 + zup), rfp.at[i, 1], zabove),
            FM0: lambda: remote(FM0, i, rows_of(i, zdown), rfm.at[i, 0], zbelow),
            FM1: lambda: remote(FM1, i, rows_of(i, 4 + zdown), rfm.at[i, 1], zbelow),
            XH: lambda: remote(XH, i, rows_of(i, 4 * (1 - xh) + z), rx.at[i], across),
        }

    def t_start(i):
        @pl.when(own)
        def _():
            t_local(i).start()

        @pl.when(jnp.logical_not(own))
        def _():
            t_copy(i).start()

    def stage_a(i):
        @pl.when(own)
        def _():
            t_local(i).wait()

        @pl.when(jnp.logical_not(own))
        def _():
            t_copy(i).wait_recv()

        c = gather_copies(i)
        for kind in (XL, UP, DN):
            c[kind]().start()

    def stage_b(i):
        c = gather_copies(i)
        c[XL]().wait_recv()
        c[UP2]().start()
        c[DN2]().start()
        c[UP]().wait_recv()
        c[UPR]().start()

    def stage_c(i):
        c = gather_copies(i)
        c[DN2]().wait_recv()
        c[DNR]().start()

    def stage_d(i):
        c = gather_copies(i)
        for kind in (DN, UP2, UPR, DNR):
            c[kind]().wait_recv()
        c[SWAP]().start()

    def convert(q):
        piece_copy(q).wait()
        v = stage[q % 2]
        hi = v.astype(BF16)
        rows = pl.ds(pl.multiple_of(q * PIECE, PIECE), PIECE)
        jhi[rows] = hi
        jlo[rows] = (v - hi.astype(F32)).astype(BF16)

        @pl.when(q + 2 < pieces)
        def _():
            piece_copy(q + 2).start()

    def stage_e(i):
        gather_copies(i)[SWAP]().wait_recv()
        for a in range(8):
            s = slot_of(jnp.int32(a), row)
            for half in range(2):
                v = xg[i, half, s]
                hi = v.astype(BF16)
                columns = slice(half * width, (half + 1) * width)
                x2[a * m : (a + 1) * m, columns] = hi
                x2[(8 + a) * m : (9 + a) * m, columns] = (v - hi.astype(F32)).astype(BF16)

        def tile(t, _):
            c = pl.ds(pl.multiple_of(t * TILE, TILE), TILE)
            both = jnp.dot(x2[...], jhi[:, c], preferred_element_type=F32)
            small = jnp.dot(x2[0 : 8 * m], jlo[:, c], preferred_element_type=F32)
            p[i, :, c] = both[: 8 * m] + (both[8 * m :] + small)
            return 0

        lax.fori_loop(0, width // TILE, tile, 0)
        c = sum_copies(i)
        for kind in (ZP, ZM, FP1, FM0):
            c[kind]().start()

    def stage_g(i):
        c = sum_copies(i)
        for kind, arrived, a, final in ((ZP, rzp, zup, FP0), (ZM, rzm, 4 + zdown, FM1)):
            c[kind]().wait_recv()
            block = rows_of(i, a)
            block[...] = block[...] + arrived[i]
            c[final]().start()

    def stage_h(i):
        c = sum_copies(i)
        for kind in (FP0, FP1, FM0, FM1):
            c[kind]().wait_recv()
        rest = 1 - xh
        block = rows_of(i, 4 * rest + z)
        block[...] = block[...] + (rfp[i, rest] + rfm[i, rest])
        c[XH]().start()
        mine = rows_of(i, 4 * xh + z)
        mine[...] = mine[...] + (rfp[i, xh] + rfm[i, xh])

    def stage_i(i):
        sum_copies(i)[XH]().wait_recv()
        out[pl.ds(pl.multiple_of(i * m, m), m)] = rows_of(i, 4 * xh + z)[...] + rx[i]

    t_start(0)
    t_start(1)
    per = pieces // 4

    def step(t, _):
        @pl.when(t + 2 < n)
        def _():
            t_start(t + 2)

        for stage_, off in (
            (stage_a, 0),
            (stage_b, 1),
            (stage_c, 2),
            (stage_d, 3),
            (stage_g, 5),
            (stage_h, 6),
            (stage_i, 7),
        ):
            i = t - off

            @pl.when(jnp.logical_and(i >= 0, i < n))
            def _():
                stage_(i)

        @pl.when(t < 4)
        def _():
            lax.fori_loop(0, per, lambda q, _: (convert(t * per + q), 0)[1], 0)

        i = t - 4

        @pl.when(jnp.logical_and(i >= 0, i < n))
        def _():
            stage_e(i)

        return 0

    lax.fori_loop(0, n + 7, step, 0)

    def drain(i, _):
        @pl.when(jnp.logical_not(own))
        def _():
            t_copy(i).wait_send()

        for c in (gather_copies(i), sum_copies(i)):
            for kind in c:
                c[kind]().wait_send()
        return 0

    lax.fori_loop(0, n, drain, 0)


def coupled_sum(positions, couplings):
    replicas, width = positions.shape
    m = replicas // CHUNKS
    n = CHUNKS
    depth = couplings.shape[0]
    vmem = pltpu.VMEM
    return pl.pallas_call(
        kernel,
        out_shape=jax.ShapeDtypeStruct((replicas, width), F32),
        in_specs=[pl.BlockSpec(memory_space=vmem), pl.BlockSpec(memory_space=pl.ANY)],
        out_specs=pl.BlockSpec(memory_space=vmem),
        scratch_shapes=[
            vmem((n, 2, 8, m, width), F32),
            vmem((depth, width), BF16),
            vmem((depth, width), BF16),
            vmem((2, PIECE, width), F32),
            vmem((16 * m, depth), BF16),
            vmem((n, 8 * m, width), F32),
            vmem((n, m, width), F32),
            vmem((n, m, width), F32),
            vmem((n, 2, m, width), F32),
            vmem((n, 2, m, width), F32),
            vmem((n, m, width), F32),
            pltpu.SemaphoreType.DMA((16, n)),
            pltpu.SemaphoreType.DMA((16, n)),
            pltpu.SemaphoreType.DMA((2,)),
        ],
        compiler_params=pltpu.CompilerParams(
            collective_id=0, has_side_effects=True, vmem_limit_bytes=66000000
        ),
    )(positions, couplings)


def per_device(positions, momenta, couplings):
    coupled = coupled_sum(positions, couplings)
    radius = positions * positions + momenta * momenta
    momenta_next = momenta + time_step * (
        -(kerr_rate * radius - pump_rate + detuning) * positions + coupling_gain * coupled
    )
    radius_next = positions * positions + momenta_next * momenta_next
    positions_next = (
        positions + time_step * (kerr_rate * radius_next + pump_rate + detuning) * momenta_next
    )
    return (positions_next, momenta_next)


def solution(mesh):
    placed = (P("row", "col"), P("row", "col"), P("row", "col"))
    return jax.shard_map(
        per_device,
        mesh=mesh,
        in_specs=placed,
        out_specs=(P("row", "col"), P("row", "col")),
        check_vma=False,
    )
```

time: 561 us -> 147 us (0.26)
  the two profiles are of different devices: /device:TPU:0 before, /device:TPU:18 now
where the time goes in v1:
time: 147 us
  Pallas kernels  144 us (98%)
  other arithmetic  2.92 us (2%)
    pallas_call x1, Pallas kernels, coupled_sum(): pl.pallas_call(kernel, out_shape=jax.ShapeDtypeStruct((replicas, width),...  144 us

profile of v1, /device:TPU:18, one launch (start us, length us, event | category | flops | bytes accessed | tf_op | source)
XLA Modules:
  0.0 147.1 jit_solution(13346300374184689888)
XLA Ops:
  0.6 0.0 copy-start
  0.6 143.5 %shard_map.50 = f32[128,1536]{1,0:T(8,128)} custom-call(f32[128,1536]{1,0:T(8,128)} %pos.1, f32[3072,1536]{1,0:T(8,128)} %coup.1), custom_call_target="tpu_custom_call" | custom-call | tf_op jit(solution)/shard_map/pallas_call | solution.py:285
  144.2 0.0 copy-done
  144.2 2.9 %multiply_add_fusion = (f32[128,1536]{1,0:T(8,128)}, f32[128,1536]{1,0:T(8,128)}) fusion(f32[128,1536]{1,0:T(8,128)S(1)} %copy-done, f32[128,1536]{1,0:T(8,128)} %param.4, f32[128,1536]{1,0:T(8,128)} %shard_map.50), kind=kLoop, calls=%fused_computation | loop fusion | flops 3145728 | bytes 3932160 | tf_op jit(solution)/shard_map/add | solution.py:320
Async XLA Ops:
  0.6 143.5 %copy-start = (f32[128,1536]{1,0:T(8,128)S(1)}, f32[128,1536]{1,0:T(8,128)}, u32[]{:S(2)}) copy-start(f32[128,1536]{1,0:T(8,128)} %pos.1) | copy-start | bytes 2359300

commit v2 on v1

--- a/solution.py
+++ b/solution.py
@@ -17,13 +17,16 @@
 CHUNKS = 8
 PIECE = 384
 TILE = 512
+AHEAD = 1
+OFF_T = 0
+OFF_B, OFF_UP, OFF_DOWN, OFF_D, OFF_E, OFF_G, OFF_H, OFF_I = 2, 3, 5, 7, 9, 14, 17, 20
 (T, XL, UP, UP2, DN, DN2, UPR, DNR, SWAP, ZP, ZM, FP0, FP1, FM0, FM1, XH) = range(16)
 
 
-def slot_of(a, b):
+def slot_of(a, b, core):
     xh, z = a // 4, a % 4
     y, xl = b // 2, b % 2
-    return 2 * ((z + 2 * y + xl) % 4) + (xh + z // 2) % 2
+    return 2 * ((z + 2 * xl + xh) % 4) + (xh + y) % 2
 
 
 def kernel(
@@ -41,12 +44,12 @@
     def at(row_, y_, xl_, core_):
         return {"row": row_, "col": (2 * y_ + xl_) * 2 + core_}
 
-    t_slot = slot_of(row, slot)
+    t_slot = slot_of(row, slot, core)
     t_to = {"row": slot, "col": t_slot * 2 + core}
     own = jnp.logical_and(slot == row, t_slot == slot)
     t_from = 0
     for a in range(8):
-        t_from = t_from + jnp.where(slot_of(jnp.int32(a), row) == slot, a, 0)
+        t_from = t_from + jnp.where(slot_of(jnp.int32(a), row, core) == slot, a, 0)
     side = at(row, y, 1 - xl, core)
     above, below = at(row, up, xl, core), at(row, down, xl, core)
     twin = at(row, y, xl, 1 - core)
@@ -135,6 +138,11 @@
         def _():
             t_copy(i).start()
 
+    def t_next(i):
+        @pl.when(i + AHEAD < n)
+        def _():
+            t_start(i + AHEAD)
+
     def stage_a(i):
         @pl.when(own)
         def _():
@@ -153,10 +161,13 @@
         c[XL]().wait_recv()
         c[UP2]().start()
         c[DN2]().start()
+
+    def stage_up(i):
+        c = gather_copies(i)
         c[UP]().wait_recv()
         c[UPR]().start()
 
-    def stage_c(i):
+    def stage_down(i):
         c = gather_copies(i)
         c[DN2]().wait_recv()
         c[DNR]().start()
@@ -179,25 +190,25 @@
         def _():
             piece_copy(q + 2).start()
 
-    def stage_e(i):
+    def stage_split(i):
         gather_copies(i)[SWAP]().wait_recv()
-        for a in range(8):
-            s = slot_of(jnp.int32(a), row)
+        for a in range(0, 8, 2):
             for half in range(2):
-                v = xg[i, half, s]
+                v = jnp.concatenate(
+                    [xg[i, half, slot_of(jnp.int32(a + d), row, half)] for d in range(2)], axis=0
+                )
                 hi = v.astype(BF16)
                 columns = slice(half * width, (half + 1) * width)
-                x2[a * m : (a + 1) * m, columns] = hi
-                x2[(8 + a) * m : (9 + a) * m, columns] = (v - hi.astype(F32)).astype(BF16)
-
-        def tile(t, _):
-            c = pl.ds(pl.multiple_of(t * TILE, TILE), TILE)
-            both = jnp.dot(x2[...], jhi[:, c], preferred_element_type=F32)
-            small = jnp.dot(x2[0 : 8 * m], jlo[:, c], preferred_element_type=F32)
-            p[i, :, c] = both[: 8 * m] + (both[8 * m :] + small)
-            return 0
-
-        lax.fori_loop(0, width // TILE, tile, 0)
+                x2[a * m : (a + 2) * m, columns] = hi
+                x2[(8 + a) * m : (10 + a) * m, columns] = (v - hi.astype(F32)).astype(BF16)
+
+    def stage_tile(t, i):
+        c = pl.ds(pl.multiple_of(t * TILE, TILE), TILE)
+        both = jnp.dot(x2[...], jhi[:, c], preferred_element_type=F32)
+        small = jnp.dot(x2[0 : 8 * m], jlo[:, c], preferred_element_type=F32)
+        p[i, :, c] = both[: 8 * m] + (both[8 * m :] + small)
+
+    def stage_f(i):
         c = sum_copies(i)
         for kind in (ZP, ZM, FP1, FM0):
             c[kind]().start()
@@ -225,43 +236,44 @@
         sum_copies(i)[XH]().wait_recv()
         out[pl.ds(pl.multiple_of(i * m, m), m)] = rows_of(i, 4 * xh + z)[...] + rx[i]
 
-    t_start(0)
-    t_start(1)
-    per = pieces // 4
-
-    def step(t, _):
-        @pl.when(t + 2 < n)
-        def _():
-            t_start(t + 2)
-
-        for stage_, off in (
-            (stage_a, 0),
-            (stage_b, 1),
-            (stage_c, 2),
-            (stage_d, 3),
-            (stage_g, 5),
-            (stage_h, 6),
-            (stage_i, 7),
-        ):
-            i = t - off
-
-            @pl.when(jnp.logical_and(i >= 0, i < n))
+    stages = (
+        (OFF_T, t_next),
+        (0, stage_a),
+        (OFF_B, stage_b),
+        (OFF_UP, stage_up),
+        (OFF_DOWN, stage_down),
+        (OFF_D, stage_d),
+        (OFF_E + 3, stage_f),
+        (OFF_G, stage_g),
+        (OFF_H, stage_h),
+        (OFF_I, stage_i),
+        (OFF_E, stage_split),
+    )
+    last = max(off for off, _ in stages)
+    for i in range(AHEAD):
+        t_start(i)
+
+    def step(u, _):
+        for off, stage_ in stages:
+            i = (u - off) // 3
+
+            @pl.when(jnp.logical_and(u >= off, jnp.logical_and(i < n, (u - off) % 3 == 0)))
             def _():
                 stage_(i)
 
-        @pl.when(t < 4)
-        def _():
-            lax.fori_loop(0, per, lambda q, _: (convert(t * per + q), 0)[1], 0)
-
-        i = t - 4
-
-        @pl.when(jnp.logical_and(i >= 0, i < n))
-        def _():
-            stage_e(i)
+        i = (u - OFF_E) // 3
+
+        @pl.when(jnp.logical_and(u >= OFF_E, i < n))
+        def _():
+            stage_tile((u - OFF_E) % 3, i)
+
+        @pl.when(u < pieces)
+        def _():
+            convert(u)
 
         return 0
 
-    lax.fori_loop(0, n + 7, step, 0)
+    lax.fori_loop(0, 3 * (n - 1) + last + 1, step, 0)
 
     def drain(i, _):
         @pl.when(jnp.logical_not(own))

time: 147 us -> 118 us (0.80)
  the two profiles are of different devices: /device:TPU:18 before, /device:TPU:0 now
where the time goes in v2:
time: 118 us; the launch traced here: 117 us
  Pallas kernels  113 us (96%)
  other arithmetic  2.92 us (2%)
    pallas_call x1, Pallas kernels, coupled_sum(): pl.pallas_call(kernel, out_shape=jax.ShapeDtypeStruct((replicas, width),...  113 us
    add x1, other arithmetic, per_device(): positions + time_step * (kerr_rate * radius_next + pump_rate + detuning)...  2.92 us

profile of v2, /device:TPU:0, one launch (start us, length us, event | category | flops | bytes accessed | tf_op | source)
XLA Modules:
  0.0 117.1 jit_solution(16427311593169466823)
XLA Ops:
  0.6 0.0 copy-start
  0.6 113.5 %shard_map.50 = f32[128,1536]{1,0:T(8,128)} custom-call(f32[128,1536]{1,0:T(8,128)} %pos.1, f32[3072,1536]{1,0:T(8,128)} %coup.1), custom_call_target="tpu_custom_call" | custom-call | tf_op jit(solution)/shard_map/pallas_call | solution.py:297
  114.1 0.0 copy-done
  114.1 2.9 %multiply_add_fusion = (f32[128,1536]{1,0:T(8,128)}, f32[128,1536]{1,0:T(8,128)}) fusion(f32[128,1536]{1,0:T(8,128)S(1)} %copy-done, f32[128,1536]{1,0:T(8,128)} %param.4, f32[128,1536]{1,0:T(8,128)} %shard_map.50), kind=kLoop, calls=%fused_computation | loop fusion | flops 3145728 | bytes 3932160 | tf_op jit(solution)/shard_map/add | solution.py:332
Async XLA Ops:
  0.6 113.5 %copy-start = (f32[128,1536]{1,0:T(8,128)S(1)}, f32[128,1536]{1,0:T(8,128)}, u32[]{:S(2)}) copy-start(f32[128,1536]{1,0:T(8,128)} %pos.1) | copy-start | bytes 2359300

commit v3 on v2

--- a/solution.py
+++ b/solution.py
@@ -17,20 +17,20 @@
 CHUNKS = 8
 PIECE = 384
 TILE = 512
-AHEAD = 1
+AHEAD = 3
 OFF_T = 0
-OFF_B, OFF_UP, OFF_DOWN, OFF_D, OFF_E, OFF_G, OFF_H, OFF_I = 2, 3, 5, 7, 9, 14, 17, 20
-(T, XL, UP, UP2, DN, DN2, UPR, DNR, SWAP, ZP, ZM, FP0, FP1, FM0, FM1, XH) = range(16)
+OFF_B, OFF_UP, OFF_DOWN, OFF_D, OFF_E, OFF_G, OFF_H, OFF_I = 3, 3, 6, 9, 11, 16, 19, 22
+(T, XL, UP, UP2, DN, DN2, UPR, DNR, SWAP, ZP, ZM, FP0, FP1, FM0, FM1, XH, T1, XL2) = range(18)
 
 
 def slot_of(a, b, core):
     xh, z = a // 4, a % 4
     y, xl = b // 2, b % 2
-    return 2 * ((z + 2 * xl + xh) % 4) + (xh + y) % 2
+    return 2 * ((2 * core + z + 4 - y + xh) % 4) + (xh + y + xl) % 2
 
 
 def kernel(
-    pos, coup, out, xg, jhi, jlo, stage, x2, p, rzp, rzm, rfp, rfm, rx, send, recv, stage_sem
+    pos, coup, out, xg, turned, jhi, jlo, stage, x2, p, rzp, rzm, rfp, rfm, rx, send, recv, stage_sem
 ):
     n, _, _, m, width = xg.shape
     row, col = lax.axis_index("row"), lax.axis_index("col")
@@ -44,12 +44,17 @@
     def at(row_, y_, xl_, core_):
         return {"row": row_, "col": (2 * y_ + xl_) * 2 + core_}
 
-    t_slot = slot_of(row, slot, core)
-    t_to = {"row": slot, "col": t_slot * 2 + core}
-    own = jnp.logical_and(slot == row, t_slot == slot)
+    turn = (2 * core + z + 4 - y + xh) % 4
+    turn_to = at(row, turn, xl, core)
+    stays = turn == y
+    t_block = 2 * turn + xl
+    t_slot = slot_of(row, t_block, core)
+    t_to = {"row": t_block, "col": t_slot * 2 + core}
+    own = jnp.logical_and(t_block == row, t_slot == slot)
     t_from = 0
     for a in range(8):
         t_from = t_from + jnp.where(slot_of(jnp.int32(a), row, core) == slot, a, 0)
+    beyond = at(row, (y + 2) % 4, xl, core)
     side = at(row, y, 1 - xl, core)
     above, below = at(row, up, xl, core), at(row, down, xl, core)
     twin = at(row, y, xl, 1 - core)
@@ -66,19 +71,19 @@
     piece_copy(1).start()
 
     barrier = pltpu.get_barrier_semaphore()
-    for other in (side, above, below, twin, zabove, zbelow, across):
+    for other in (side, above, below, beyond, twin, zabove, zbelow, across):
         pl.semaphore_signal(barrier, inc=1, device_id=other, device_id_type=MESH)
 
     @pl.when(jnp.logical_not(own))
     def _():
         pl.semaphore_signal(
-            barrier, inc=1, device_id={"row": t_from, "col": row * 2 + core}, device_id_type=MESH
+            barrier, inc=1, device_id=at(t_from, y, row % 2, core), device_id_type=MESH
         )
-        pl.semaphore_wait(barrier, 8)
+        pl.semaphore_wait(barrier, 9)
 
     @pl.when(own)
     def _():
-        pl.semaphore_wait(barrier, 7)
+        pl.semaphore_wait(barrier, 8)
 
     def remote(kind, i, src, dst, to):
         return pltpu.make_async_remote_copy(
@@ -96,14 +101,24 @@
     def t_src(i):
         return pos.at[pl.ds(pl.multiple_of(i * m, m), m)]
 
+    def turn_copy(i):
+        return remote(T1, i, t_src(i), turned.at[i], turn_to)
+
+    def turn_local(i):
+        return pltpu.make_async_copy(t_src(i), turned.at[i], recv.at[T1, i])
+
     def t_copy(i):
-        return remote(T, i, t_src(i), xg.at[i, core, t_slot], t_to)
+        return remote(T, i, turned.at[i], xg.at[i, core, t_slot], t_to)
 
     def t_local(i):
-        return pltpu.make_async_copy(t_src(i), xg.at[i, core, slot], recv.at[T, i])
+        return pltpu.make_async_copy(turned.at[i], xg.at[i, core, slot], recv.at[T, i])
 
     def gather_copy(kind, i, slot_, to):
         block = xg.at[i, core, slot_]
+        return remote(kind, i, block, block, to)
+
+    def half_copy(kind, i, slot_, half, to):
+        block = xg.at[i, core, slot_, pl.ds(half * (m // 2), m // 2)]
         return remote(kind, i, block, block, to)
 
     def gather_copies(i):
@@ -113,8 +128,9 @@
             DN: lambda: gather_copy(DN, i, slot, below),
             UP2: lambda: gather_copy(UP2, i, 2 * y + 1 - xl, above),
             DN2: lambda: gather_copy(DN2, i, 2 * y + 1 - xl, below),
-            UPR: lambda: gather_copy(UPR, i, 2 * down + xl, above),
-            DNR: lambda: gather_copy(DNR, i, 2 * up + 1 - xl, below),
+            UPR: lambda: half_copy(UPR, i, 2 * down + xl, 0, above),
+            DNR: lambda: half_copy(DNR, i, 2 * up + xl, 1, below),
+            XL2: lambda: gather_copy(XL2, i, 2 * ((y + 2) % 4) + xl, side),
             SWAP: lambda: remote(SWAP, i, xg.at[i, core], xg.at[i, core], twin),
         }
 
@@ -129,7 +145,24 @@
             XH: lambda: remote(XH, i, rows_of(i, 4 * (1 - xh) + z), rx.at[i], across),
         }
 
+    def turn_start(i):
+        @pl.when(stays)
+        def _():
+            turn_local(i).start()
+
+        @pl.when(jnp.logical_not(stays))
+        def _():
+            turn_copy(i).start()
+
     def t_start(i):
+        @pl.when(stays)
+        def _():
+            turn_local(i).wait()
+
+        @pl.when(jnp.logical_not(stays))
+        def _():
+            turn_copy(i).wait_recv()
+
         @pl.when(own)
         def _():
             t_local(i).start()
@@ -137,6 +170,11 @@
         @pl.when(jnp.logical_not(own))
         def _():
             t_copy(i).start()
+
+    def turn_next(i):
+        @pl.when(i + AHEAD + 1 < n)
+        def _():
+            turn_start(i + AHEAD + 1)
 
     def t_next(i):
         @pl.when(i + AHEAD < n)
@@ -166,15 +204,18 @@
         c = gather_copies(i)
         c[UP]().wait_recv()
         c[UPR]().start()
+        c[DN]().wait_recv()
+        c[DNR]().start()
 
     def stage_down(i):
         c = gather_copies(i)
-        c[DN2]().wait_recv()
-        c[DNR]().start()
+        c[UPR]().wait_recv()
+        c[DNR]().wait_recv()
+        c[XL2]().start()
 
     def stage_d(i):
         c = gather_copies(i)
-        for kind in (DN, UP2, UPR, DNR):
+        for kind in (UP2, DN2, XL2):
             c[kind]().wait_recv()
         c[SWAP]().start()
 
@@ -237,8 +278,9 @@
         out[pl.ds(pl.multiple_of(i * m, m), m)] = rows_of(i, 4 * xh + z)[...] + rx[i]
 
     stages = (
+        (0, turn_next),
+        (0, stage_a),
         (OFF_T, t_next),
-        (0, stage_a),
         (OFF_B, stage_b),
         (OFF_UP, stage_up),
         (OFF_DOWN, stage_down),
@@ -250,6 +292,8 @@
         (OFF_E, stage_split),
     )
     last = max(off for off, _ in stages)
+    for i in range(AHEAD + 1):
+        turn_start(i)
     for i in range(AHEAD):
         t_start(i)
 
@@ -279,6 +323,10 @@
         @pl.when(jnp.logical_not(own))
         def _():
             t_copy(i).wait_send()
+
+        @pl.when(jnp.logical_not(stays))
+        def _():
+            turn_copy(i).wait_send()
 
         for c in (gather_copies(i), sum_copies(i)):
             for kind in c:
@@ -301,6 +349,7 @@
         out_specs=pl.BlockSpec(memory_space=vmem),
         scratch_shapes=[
             vmem((n, 2, 8, m, width), F32),
+            vmem((n, m, width), F32),
             vmem((depth, width), BF16),
             vmem((depth, width), BF16),
             vmem((2, PIECE, width), F32),
@@ -311,8 +360,8 @@
             vmem((n, 2, m, width), F32),
             vmem((n, 2, m, width), F32),
             vmem((n, m, width), F32),
-            pltpu.SemaphoreType.DMA((16, n)),
-            pltpu.SemaphoreType.DMA((16, n)),
+            pltpu.SemaphoreType.DMA((18, n)),
+            pltpu.SemaphoreType.DMA((18, n)),
             pltpu.SemaphoreType.DMA((2,)),
         ],
         compiler_params=pltpu.CompilerParams(

time: 118 us -> 111 us (0.941)
  Pallas kernels: 113 us -> 107 us
    pallas_call x1, Pallas kernels: 113 us -> 107 us  [coupled_sum(): pl.pallas_call(kernel, out_shape=jax.ShapeDtypeStruct((replicas, width),...]
where the time goes in v3:
time: 111 us; the launch traced here: 110 us
  Pallas kernels  107 us (96%)
  other arithmetic  2.92 us (3%)
    pallas_call x1, Pallas kernels, coupled_sum(): pl.pallas_call(kernel, out_shape=jax.ShapeDtypeStruct((replicas, width),...  107 us
    add x1, other arithmetic, per_device(): positions + time_step * (kerr_rate * radius_next + pump_rate + detuning)...  2.92 us

profile of v3, /device:TPU:0, one launch (start us, length us, event | category | flops | bytes accessed | tf_op | source)
XLA Modules:
  0.0 110.4 jit_solution(7204724968104139339)
XLA Ops:
  0.6 0.0 copy-start
  0.6 106.8 %shard_map.50 = f32[128,1536]{1,0:T(8,128)} custom-call(f32[128,1536]{1,0:T(8,128)} %pos.1, f32[3072,1536]{1,0:T(8,128)} %coup.1), custom_call_target="tpu_custom_call" | custom-call | tf_op jit(solution)/shard_map/pallas_call | solution.py:345
  107.5 0.0 copy-done
  107.5 2.9 %multiply_add_fusion = (f32[128,1536]{1,0:T(8,128)}, f32[128,1536]{1,0:T(8,128)}) fusion(f32[128,1536]{1,0:T(8,128)S(1)} %copy-done, f32[128,1536]{1,0:T(8,128)} %param.4, f32[128,1536]{1,0:T(8,128)} %shard_map.50), kind=kLoop, calls=%fused_computation | loop fusion | flops 3145728 | bytes 3932160 | tf_op jit(solution)/shard_map/add | solution.py:381
Async XLA Ops:
  0.6 106.9 %copy-start = (f32[128,1536]{1,0:T(8,128)S(1)}, f32[128,1536]{1,0:T(8,128)}, u32[]{:S(2)}) copy-start(f32[128,1536]{1,0:T(8,128)} %pos.1) | copy-start | bytes 2359300

commit v4 on v3

--- a/solution.py
+++ b/solution.py
@@ -19,7 +19,7 @@
 TILE = 512
 AHEAD = 3
 OFF_T = 0
-OFF_B, OFF_UP, OFF_DOWN, OFF_D, OFF_E, OFF_G, OFF_H, OFF_I = 3, 3, 6, 9, 11, 16, 19, 22
+OFF_B, OFF_UP, OFF_DOWN, OFF_D, OFF_E, OFF_G, OFF_H, OFF_I = 3, 3, 6, 9, 11, 18, 22, 26
 (T, XL, UP, UP2, DN, DN2, UPR, DNR, SWAP, ZP, ZM, FP0, FP1, FM0, FM1, XH, T1, XL2) = range(18)
 
 
@@ -136,14 +136,19 @@
 
     def sum_copies(i):
         return {
-            ZP: lambda: remote(ZP, i, rows_of(i, zfar), rzp.at[i], zabove),
-            ZM: lambda: remote(ZM, i, rows_of(i, 4 + zfar), rzm.at[i], zbelow),
             FP0: lambda: remote(FP0, i, rows_of(i, zup), rfp.at[i, 0], zabove),
             FP1: lambda: remote(FP1, i, rows_of(i, 4 + zup), rfp.at[i, 1], zabove),
             FM0: lambda: remote(FM0, i, rows_of(i, zdown), rfm.at[i, 0], zbelow),
             FM1: lambda: remote(FM1, i, rows_of(i, 4 + zdown), rfm.at[i, 1], zbelow),
             XH: lambda: remote(XH, i, rows_of(i, 4 * (1 - xh) + z), rx.at[i], across),
         }
+
+    def far_copies(t, i):
+        c = pl.ds(pl.multiple_of(t * TILE, TILE), TILE)
+        return (
+            remote(18 + t, i, rows_of(i, zfar).at[:, c], rzp.at[i, :, c], zabove),
+            remote(21 + t, i, rows_of(i, 4 + zfar).at[:, c], rzm.at[i, :, c], zbelow),
+        )
 
     def turn_start(i):
         @pl.when(stays)
@@ -248,16 +253,19 @@
         both = jnp.dot(x2[...], jhi[:, c], preferred_element_type=F32)
         small = jnp.dot(x2[0 : 8 * m], jlo[:, c], preferred_element_type=F32)
         p[i, :, c] = both[: 8 * m] + (both[8 * m :] + small)
+        for copy in far_copies(t, i):
+            copy.start()
 
     def stage_f(i):
         c = sum_copies(i)
-        for kind in (ZP, ZM, FP1, FM0):
+        for kind in (FP1, FM0):
             c[kind]().start()
 
     def stage_g(i):
         c = sum_copies(i)
-        for kind, arrived, a, final in ((ZP, rzp, zup, FP0), (ZM, rzm, 4 + zdown, FM1)):
-            c[kind]().wait_recv()
+        for side_, arrived, a, final in ((0, rzp, zup, FP0), (1, rzm, 4 + zdown, FM1)):
+            for t in range(3):
+                far_copies(t, i)[side_].wait_recv()
             block = rows_of(i, a)
             block[...] = block[...] + arrived[i]
             c[final]().start()
@@ -328,6 +336,9 @@
         def _():
             turn_copy(i).wait_send()
 
+        for t in range(3):
+            for copy in far_copies(t, i):
+                copy.wait_send()
         for c in (gather_copies(i), sum_copies(i)):
             for kind in c:
                 c[kind]().wait_send()
@@ -360,8 +371,8 @@
             vmem((n, 2, m, width), F32),
             vmem((n, 2, m, width), F32),
             vmem((n, m, width), F32),
-            pltpu.SemaphoreType.DMA((18, n)),
-            pltpu.SemaphoreType.DMA((18, n)),
+            pltpu.SemaphoreType.DMA((24, n)),
+            pltpu.SemaphoreType.DMA((24, n)),
             pltpu.SemaphoreType.DMA((2,)),
         ],
         compiler_params=pltpu.CompilerParams(

time: 111 us -> 110 us (level)
    pallas_call x1, Pallas kernels: 107 us -> 106 us  [coupled_sum(): pl.pallas_call(kernel, out_shape=jax.ShapeDtypeStruct((replicas, width),...]
where the time goes in v4:
time: 110 us; the launch traced here: 109 us
  Pallas kernels  106 us (96%)
  other arithmetic  2.92 us (3%)
    pallas_call x1, Pallas kernels, coupled_sum(): pl.pallas_call(kernel, out_shape=jax.ShapeDtypeStruct((replicas, width),...  106 us
    add x1, other arithmetic, per_device(): positions + time_step * (kerr_rate * radius_next + pump_rate + detuning)...  2.92 us

profile of v4, /device:TPU:0, one launch (start us, length us, event | category | flops | bytes accessed | tf_op | source)
XLA Modules:
  0.0 109.1 jit_solution(6852688079715418162)
XLA Ops:
  0.6 0.0 copy-start
  0.6 105.5 %shard_map.50 = f32[128,1536]{1,0:T(8,128)} custom-call(f32[128,1536]{1,0:T(8,128)} %pos.1, f32[3072,1536]{1,0:T(8,128)} %coup.1), custom_call_target="tpu_custom_call" | custom-call | tf_op jit(solution)/shard_map/pallas_call | solution.py:356
  106.2 0.0 copy-done
  106.2 2.9 %multiply_add_fusion = (f32[128,1536]{1,0:T(8,128)}, f32[128,1536]{1,0:T(8,128)}) fusion(f32[128,1536]{1,0:T(8,128)S(1)} %copy-done, f32[128,1536]{1,0:T(8,128)} %param.4, f32[128,1536]{1,0:T(8,128)} %shard_map.50), kind=kLoop, calls=%fused_computation | loop fusion | flops 3145728 | bytes 3932160 | tf_op jit(solution)/shard_map/add | solution.py:392
Async XLA Ops:
  0.6 105.5 %copy-start = (f32[128,1536]{1,0:T(8,128)S(1)}, f32[128,1536]{1,0:T(8,128)}, u32[]{:S(2)}) copy-start(f32[128,1536]{1,0:T(8,128)} %pos.1) | copy-start | bytes 2359300

commit v5 on v4

--- a/solution.py
+++ b/solution.py
@@ -137,17 +137,17 @@
     def sum_copies(i):
         return {
             FP0: lambda: remote(FP0, i, rows_of(i, zup), rfp.at[i, 0], zabove),
-            FP1: lambda: remote(FP1, i, rows_of(i, 4 + zup), rfp.at[i, 1], zabove),
-            FM0: lambda: remote(FM0, i, rows_of(i, zdown), rfm.at[i, 0], zbelow),
             FM1: lambda: remote(FM1, i, rows_of(i, 4 + zdown), rfm.at[i, 1], zbelow),
             XH: lambda: remote(XH, i, rows_of(i, 4 * (1 - xh) + z), rx.at[i], across),
         }
 
-    def far_copies(t, i):
+    def tile_copies(t, i):
         c = pl.ds(pl.multiple_of(t * TILE, TILE), TILE)
         return (
             remote(18 + t, i, rows_of(i, zfar).at[:, c], rzp.at[i, :, c], zabove),
             remote(21 + t, i, rows_of(i, 4 + zfar).at[:, c], rzm.at[i, :, c], zbelow),
+            remote(24 + t, i, rows_of(i, 4 + zup).at[:, c], rfp.at[i, 1, :, c], zabove),
+            remote(27 + t, i, rows_of(i, zdown).at[:, c], rfm.at[i, 0, :, c], zbelow),
         )
 
     def turn_start(i):
@@ -253,27 +253,25 @@
         both = jnp.dot(x2[...], jhi[:, c], preferred_element_type=F32)
         small = jnp.dot(x2[0 : 8 * m], jlo[:, c], preferred_element_type=F32)
         p[i, :, c] = both[: 8 * m] + (both[8 * m :] + small)
-        for copy in far_copies(t, i):
+        for copy in tile_copies(t, i):
             copy.start()
-
-    def stage_f(i):
-        c = sum_copies(i)
-        for kind in (FP1, FM0):
-            c[kind]().start()
 
     def stage_g(i):
         c = sum_copies(i)
         for side_, arrived, a, final in ((0, rzp, zup, FP0), (1, rzm, 4 + zdown, FM1)):
             for t in range(3):
-                far_copies(t, i)[side_].wait_recv()
+                tile_copies(t, i)[side_].wait_recv()
             block = rows_of(i, a)
             block[...] = block[...] + arrived[i]
             c[final]().start()
 
     def stage_h(i):
         c = sum_copies(i)
-        for kind in (FP0, FP1, FM0, FM1):
+        for kind in (FP0, FM1):
             c[kind]().wait_recv()
+        for t in range(3):
+            for copy in tile_copies(t, i)[2:]:
+                copy.wait_recv()
         rest = 1 - xh
         block = rows_of(i, 4 * rest + z)
         block[...] = block[...] + (rfp[i, rest] + rfm[i, rest])
@@ -293,7 +291,6 @@
         (OFF_UP, stage_up),
         (OFF_DOWN, stage_down),
         (OFF_D, stage_d),
-        (OFF_E + 3, stage_f),
         (OFF_G, stage_g),
         (OFF_H, stage_h),
         (OFF_I, stage_i),
@@ -337,7 +334,7 @@
             turn_copy(i).wait_send()
 
         for t in range(3):
-            for copy in far_copies(t, i):
+            for copy in tile_copies(t, i):
                 copy.wait_send()
         for c in (gather_copies(i), sum_copies(i)):
             for kind in c:
@@ -371,8 +368,8 @@
             vmem((n, 2, m, width), F32),
             vmem((n, 2, m, width), F32),
             vmem((n, m, width), F32),
-            pltpu.SemaphoreType.DMA((24, n)),
-            pltpu.SemaphoreType.DMA((24, n)),
+            pltpu.SemaphoreType.DMA((30, n)),
+            pltpu.SemaphoreType.DMA((30, n)),
             pltpu.SemaphoreType.DMA((2,)),
         ],
         compiler_params=pltpu.CompilerParams(

time: 110 us -> 110 us (level)
  no operation moved by 1% of the time
where the time goes in v5:
time: 110 us; the launch traced here: 109 us
  Pallas kernels  106 us (96%)
  other arithmetic  2.92 us (3%)
    pallas_call x1, Pallas kernels, coupled_sum(): pl.pallas_call(kernel, out_shape=jax.ShapeDtypeStruct((replicas, width),...  106 us
    add x1, other arithmetic, per_device(): positions + time_step * (kerr_rate * radius_next + pump_rate + detuning)...  2.92 us

profile of v5, /device:TPU:0, one launch (start us, length us, event | category | flops | bytes accessed | tf_op | source)
XLA Modules:
  0.0 109.1 jit_solution(8984019247040053739)
XLA Ops:
  0.6 0.0 copy-start
  0.6 105.6 %shard_map.50 = f32[128,1536]{1,0:T(8,128)} custom-call(f32[128,1536]{1,0:T(8,128)} %pos.1, f32[3072,1536]{1,0:T(8,128)} %coup.1), custom_call_target="tpu_custom_call" | custom-call | tf_op jit(solution)/shard_map/pallas_call | solution.py:353
  106.2 0.0 copy-done
  106.2 2.9 %multiply_add_fusion = (f32[128,1536]{1,0:T(8,128)}, f32[128,1536]{1,0:T(8,128)}) fusion(f32[128,1536]{1,0:T(8,128)S(1)} %copy-done, f32[128,1536]{1,0:T(8,128)} %param.4, f32[128,1536]{1,0:T(8,128)} %shard_map.50), kind=kLoop, calls=%fused_computation | loop fusion | flops 3145728 | bytes 3932160 | tf_op jit(solution)/shard_map/add | solution.py:389
Async XLA Ops:
  0.6 105.6 %copy-start = (f32[128,1536]{1,0:T(8,128)S(1)}, f32[128,1536]{1,0:T(8,128)}, u32[]{:S(2)}) copy-start(f32[128,1536]{1,0:T(8,128)} %pos.1) | copy-start | bytes 2359300
